TPU v7x, 256 devices: a whole 4x4x8 slice. The times are simulated.
256 devices in a mesh: chan: 32 (over y, x, core), head: 4 (over z_lo), region: 2 (over z_hi).
Axes of the slice: x: 4, y: 4, z: 8 (z_hi: 2, z_lo: 4; z = z_hi * 4 + z_lo), core: 2. Of those that a mesh axis runs over, the one named last changes fastest.
Arguments:
- tokens: bfloat16 [512, 16, 4096], P('chan', 'region', 'head'), parts along dimension 1, may hold values from -56 to 56
- position: bfloat16 [512, 4096], P('chan', 'head'), may hold values from -3 to 3
- gain: bfloat16 [4096], P('head'), may hold values from 0.099609375 to 1.8984375
- qkv_weight: bfloat16 [3, 4096, 2048], P(None, 'chan', 'head'), may hold values from -0.09375 to 0.09375
- out_weight: bfloat16 [2048, 4096], P('head'), may hold values from -0.25 to 0.25
- cotangent: bfloat16 [512, 16, 4096], P('chan', 'region', 'head'), parts along dimension 1, may hold values from -6 to 6
Outputs:
- layer_out: bfloat16 [512, 16, 4096], P('chan', 'region', 'head'), parts along dimension 1
- input_grad: bfloat16 [512, 16, 4096], P('chan', 'region', 'head'), parts along dimension 1
There are 2 independent parts, one for each index of `region`. A program takes and returns all parts, laid end to end along the dimension named above; an argument that names none is the same for every part. Nothing has to cross between parts.
All inputs are finite; a program needn't handle non-finite values.
Results may differ from a plain program's by a relative error of at most 0.01.
Values may be sent and summed in bfloat16 or wider, within the bound.
No kernel may reach another device: no remote copies, remote signals or barrier semaphores. Data moves between devices by JAX's collectives and lax.ppermute only.
A program may use at most 64 MiB of HBM per device.

v0:
```python
import jax
import jax.numpy as jnp
from jax import lax
from jax.experimental import pallas as pl
from jax.experimental.pallas import tpu as pltpu
from jax.sharding import PartitionSpec as P


F32 = jnp.float32
BF = jnp.bfloat16
NY, NX, NC, NZ = 4, 4, 2, 4
HD = 128
FAC = HD ** -0.5
CHG = 16
PAT = 8


def chan_id(y, x, c):
    return (y % NY) * (NX * NC) + (x % NX) * NC + (c % NC)


SITES = [(y, x, c) for y in range(NY) for x in range(NX) for c in range(NC)]
SWAP = [(chan_id(y, x, c), chan_id(y, x, c + 1)) for y, x, c in SITES]
SAME_CORE = [[chan_id(y, x, c) for y in range(NY) for x in range(NX)] for c in range(NC)]


def ring(first, step):
    pairs = []
    for y, x, c in SITES:
        if (c == 0) == first:
            pairs.append((chan_id(y, x, c), chan_id(y, x + step, c)))
        else:
            pairs.append((chan_id(y, x, c), chan_id(y + step, x, c)))
    return pairs


def swap(value):
    return lax.ppermute(value, "chan", SWAP)


def zshift(value, step):
    return lax.ppermute(value, "head", [(i, (i + step) % NZ) for i in range(NZ)])


def dot_nt(a, b):
    return lax.dot_general(a, b, (((1,), (1,)), ((), ())), preferred_element_type=F32)


def dot_nn(a, b):
    return lax.dot_general(a, b, (((1,), (0,)), ((), ())), preferred_element_type=F32)


def dot_tn(a, b):
    return lax.dot_general(a, b, (((0,), (0,)), ((), ())), preferred_element_type=F32)


def inv_norm(u):
    return lax.rsqrt(jnp.mean(u * u, axis=-1, keepdims=True) + 1e-06)


def norm_back(u, r, dy):
    return r * dy - u * (r * r * r * jnp.mean(dy * u, axis=-1, keepdims=True))


def same_patch(rows, cols):
    ri = lax.broadcasted_iota(jnp.int32, (rows, cols), 0) % PAT
    ci = lax.broadcasted_iota(jnp.int32, (rows, cols), 1) % PAT
    return ri == ci


def softmax_rows(scores, mask):
    e = jnp.where(mask, jnp.exp(scores), 0.0)
    return e * (1.0 / jnp.sum(e, axis=-1, keepdims=True))


def place():
    chan = lax.axis_index("chan")
    return chan // 8, (chan // 2) % 4, chan % 2, lax.axis_index("head")


def slot_of(off):
    return jnp.where(off == 3, 1, jnp.where(off == 1, 2, jnp.where(off == 2, 3, 0)))


def within(proj, rows, h, mask):
    q = proj[rows, pl.ds(h * 128, 128)]
    k = proj[rows, pl.ds(256 + h * 128, 128)]
    v = proj[rows, pl.ds(512 + h * 128, 128)]
    qf = q.astype(F32)
    kf = k.astype(F32)
    rq = inv_norm(qf)
    rk = inv_norm(kf)
    kn = (kf * rk).astype(BF)
    w = softmax_rows(dot_nt(q, kn) * (rq * FAC), mask)
    return qf, kf, v, rq, rk, kn, w


def prepare_kernel(tokens, position, gain, message, tok, pos, gn, sems):
    copies = [
        pltpu.make_async_copy(tokens, tok, sems.at[0]),
        pltpu.make_async_copy(position, pos, sems.at[1]),
        pltpu.make_async_copy(gain, gn, sems.at[2]),
    ]
    for copy in copies:
        copy.start()
    for copy in copies:
        copy.wait()
    hidden = tok[...].astype(F32) + pos[...].astype(F32)[:, None, :]
    message[0:128, :] = hidden.reshape(128, 1024).astype(BF)
    message[128:136, :] = jnp.broadcast_to(gn[...][None], (8, 1024))


def norm_kernel(p0, p1, p2, p3, normed, inv):
    parts = (p0, p1, p2, p3)
    square = jnp.zeros((128, 1), F32)
    for p in parts:
        h = p[0:128, :].astype(F32)
        square = square + jnp.sum(h * h, axis=-1, keepdims=True)
    r = lax.rsqrt(square * (1.0 / 4096) + 1e-05)
    inv[...] = jnp.broadcast_to(r, (128, 128))
    for n, p in enumerate(parts):
        for b in range(4):
            cols = pl.ds(b * 256, 256)
            h = p[0:128, cols].astype(F32)
            g = p[128:136, cols].astype(F32)[0:1]
            normed[n * 4 + b] = (h * r * g).astype(BF)


EARLY = ((0, 1), (1, 2), (3, 1), (4, 1), (8, 1), (5, 2), (9, 2), (7, 1), (11, 1))
LATE = ((0, "a"), (0, "b"), (1, 1), (2, 1), (3, "a"), (3, "b"))


def save_pieces(pieces, places, wall, base, sems):
    copies = []
    for n, (ref, (slot, size)) in enumerate(zip(pieces, places)):
        if size == "a":
            dst = wall.at[base + slot, 0:1]
        elif size == "b":
            dst = wall.at[base + slot, 1:2]
        else:
            dst = wall.at[base + slot:base + slot + size]
        copy = pltpu.make_async_copy(ref, dst, sems.at[n])
        copy.start()
        copies.append(copy)
    return copies


def rows_of(pieces, j):
    parts = []
    for ref in pieces:
        if len(ref.shape) == 4:
            parts.append(ref[0, j])
        else:
            parts.append(ref[:, :, j].reshape(-1, 256))
    return jnp.concatenate(parts, 0)


def group_lhs(own, oth, s3):
    y, x, core, z = place()
    lead = core == 0
    parts = []
    for s1 in (0, 3, 1, 2):
        by = (y + jnp.where(lead, s3, s1)) % 4
        bx = (x + jnp.where(lead, s1, s3)) % 4
        blk = ((z + 4 - by) % 4) * 4 + bx
        parts.append(jnp.concatenate([own[blk], oth[blk]], 0))
    return jnp.concatenate(parts, 1)


def project_early_kernel(own, oth, *refs):
    pieces = refs[:9]
    acc, wall, sems = refs[9:]
    copies = save_pieces(pieces, EARLY, wall, 0, sems)
    for n, group in enumerate(((0, 1, 2), (3, 5, 7), (4, 6, 8))):
        lhs = group_lhs(own, oth, (0, 3, 1)[n])
        for j in range(3):
            cols = slice(j * 256, (j + 1) * 256)
            r = dot_nn(lhs, rows_of([pieces[at] for at in group], j))
            if n == 0:
                acc[:, cols] = r
            else:
                acc[:, cols] += r
    for copy in copies:
        copy.wait()


def project_late_kernel(own, oth, acc, wall_in, *refs):
    pieces = refs[:6]
    proj, agg, wall, sems = refs[6:]
    copies = save_pieces(pieces, LATE, wall, 12, sems)
    lhs = group_lhs(own, oth, 2)
    for j in range(3):
        cols = slice(j * 256, (j + 1) * 256)
        r = dot_nn(lhs, rows_of(pieces, j))
        proj[:, cols] = (acc[:, cols] + r).astype(BF)
    mask = same_patch(128, 128)
    where = [(g, h) for g in range(2) for h in range(2)]
    firsts = first_step(proj, where, mask)
    for (g, h), f in zip(where, firsts):
        m = jnp.sum(f.reshape(CHG, PAT, HD), axis=0) * (1.0 / CHG)
        agg[:, h, pl.ds(g * PAT, PAT), :] = jnp.broadcast_to(m.astype(BF)[None], (16, PAT, HD))
    for copy in copies:
        copy.wait()


def first_step(proj, where, mask):
    def part(g, h, j):
        return proj[pl.ds(g * 128, 128), pl.ds(j * 256 + h * 128, 128)]

    qs = [part(g, h, 0) for g, h in where]
    ks = [part(g, h, 1).astype(F32) for g, h in where]
    kns = [(k * inv_norm(k)).astype(BF) for k in ks]
    rqs = [inv_norm(q.astype(F32)) * FAC for q in qs]
    scores = [dot_nt(q, kn) * rq for q, kn, rq in zip(qs, kns, rqs)]
    ws = [softmax_rows(sc, mask).astype(BF) for sc in scores]
    return [dot_nn(w, part(g, h, 2)) for w, (g, h) in zip(ws, where)]


def across_kernel(proj, agg, mix_own, mix_oth, soft):
    mask = same_patch(256, 256)
    small = same_patch(128, 128)
    where = [(g, h) for h in range(2) for g in range(2)]
    seconds = []
    for h in range(2):
        q = proj[:, pl.ds(h * 128, 128)]
        rq = inv_norm(q.astype(F32))
        a = agg[:, h].reshape(256, HD)
        af = a.astype(F32)
        an = (af * inv_norm(af)).astype(BF)
        w = softmax_rows(dot_nt(q, an) * (rq * FAC), mask)
        soft[h] = w
        seconds.append(dot_nn(w.astype(BF), a))
    firsts = first_step(proj, where, small)
    for (g, h), first in zip(where, firsts):
        ref = (mix_own, mix_oth)[g]
        ref[:, pl.ds(h * 128, 128)] = (first + seconds[h][g * 128:(g + 1) * 128]).astype(BF)


def across_back_kernel(proj, agg, gm_mine, gm_got, soft, gg, gagg):
    for h in range(2):
        cols = pl.ds(h * 128, 128)
        qf = proj[:, cols].astype(F32)
        rq = inv_norm(qf)
        a = agg[:, h].reshape(256, HD)
        af = a.astype(F32)
        ra = inv_norm(af)
        an = (af * ra).astype(BF)
        w = soft[h]
        wb = w.astype(BF)
        gf = jnp.concatenate([gm_mine[:, cols], gm_got[:, cols]], 0)
        g = gf.astype(BF)
        dw = dot_nt(g, a)
        wdw = w * dw
        dsb = ((wdw - w * jnp.sum(wdw, axis=-1, keepdims=True)) * FAC).astype(BF)
        gg[:, cols] = gf
        gg[:, pl.ds(256 + h * 128, 128)] = norm_back(qf, rq, dot_nn(dsb, an))
        dan = dot_tn(dsb, (qf * rq).astype(BF))
        da = dot_tn(wb, g) + norm_back(af, ra, dan)
        gagg[:, h] = da.astype(BF).reshape(16, 16, HD)


def quarter_slots(d):
    y, x, core, z = place()
    by = (z + d) % 4
    py = slot_of((by + 4 - y) % 4)
    slots = []
    for bx in range(4):
        px = slot_of((bx + 4 - x) % 4)
        slots.append(jnp.where(core == 0, py * 4 + px, px * 4 + py))
    return slots


def fetch(wall, wv, sems, d, at):
    copies = []
    for bx, slot in enumerate(quarter_slots(d)):
        copy = pltpu.make_async_copy(wall.at[slot], wv.at[at + bx], sems.at[at + bx])
        copy.start()
        copies.append(copy)
    return copies


def block_product(stk, wv, n):
    w = jnp.concatenate([wv[n, :, j].reshape(256, 256) for j in range(3)], 1)
    return dot_nt(stk[...], w)


def back_kernel(proj, gg, ragg, wall, own, oth, stk, corr_own, corr_oth, wv, sems):
    copies = fetch(wall, wv, sems, 2, 0)
    own_grad = jnp.sum(ragg[...].astype(F32), axis=0) * (1.0 / CHG)
    mask = same_patch(128, 128)
    where = [(g, h) for g in range(2) for h in range(2)]
    fwd = [within(proj, pl.ds(g * 128, 128), h, mask) for g, h in where]
    grads = []
    for g, h in where:
        og = own_grad[h, g * PAT:(g + 1) * PAT, :]
        gf = gg[pl.ds(g * 128, 128), pl.ds(h * 128, 128)]
        grads.append((gf + jnp.broadcast_to(og[None], (CHG, PAT, HD)).reshape(128, HD)).astype(BF))
    dws = [dot_nt(gb, f[2]) for gb, f in zip(grads, fwd)]
    dvs = [dot_tn(f[6].astype(BF), gb).astype(BF) for gb, f in zip(grads, fwd)]
    dss = []
    for f, dw in zip(fwd, dws):
        wdw = f[6] * dw
        dss.append(((wdw - f[6] * jnp.sum(wdw, axis=-1, keepdims=True)) * FAC).astype(BF))
    dqs = [dot_nn(ds, f[5]) for ds, f in zip(dss, fwd)]
    dks = [dot_tn(ds, (f[0] * f[3]).astype(BF)) for ds, f in zip(dss, fwd)]
    totals = [jnp.zeros((128, 1), F32), jnp.zeros((128, 1), F32)]
    for n, (g, h) in enumerate(where):
        qf, kf, v, rq, rk, _, _ = fwd[n]
        rows = pl.ds(g * 128, 128)
        dq = (norm_back(qf, rq, dqs[n]) + gg[rows, pl.ds(256 + h * 128, 128)]).astype(BF)
        dk = norm_back(kf, rk, dks[n]).astype(BF)
        stk[rows, pl.ds(h * 128, 128)] = dq
        stk[rows, pl.ds(256 + h * 128, 128)] = dk
        stk[rows, pl.ds(512 + h * 128, 128)] = dvs[n]
        prod = dq.astype(F32) * qf + dk.astype(F32) * kf + dvs[n].astype(F32) * v.astype(F32)
        totals[g] = totals[g] + jnp.sum(prod, axis=-1, keepdims=True)
    corr_own[...] = jnp.broadcast_to(totals[0], (128, 128))
    corr_oth[...] = jnp.broadcast_to(totals[1], (128, 128))
    for copy in copies:
        copy.wait()

    def step(bx, carry):
        r = block_product(stk, wv, bx)
        cols = pl.ds(pl.multiple_of(bx * 256, 256), 256)
        own[:, cols] = r[0:128].astype(BF)
        oth[:, cols] = r[128:256].astype(BF)
        return carry

    lax.fori_loop(0, 4, step, 0)


def side_kernel(stk, wall, own, oth, wv, sems):
    copies = []
    for n, d in enumerate((1, 3)):
        copies.append(fetch(wall, wv, sems, d, n * 4))
    for n in range(2):
        for copy in copies[n]:
            copy.wait()

        def step(bx, carry):
            r = block_product(stk, wv, n * 4 + bx)
            cols = pl.ds(pl.multiple_of(bx * 256, 256), 256)
            own[n, :, cols] = r[0:128].astype(BF)
            oth[n, :, cols] = r[128:256].astype(BF)
            return carry

        lax.fori_loop(0, 4, step, 0)


def home_kernel(stk, wall, own, oth, wv, sems):
    for copy in fetch(wall, wv, sems, 0, 0):
        copy.wait()

    def step(bx, carry):
        r = block_product(stk, wv, bx)
        cols = pl.ds(pl.multiple_of(bx * 256, 256), 256)
        own[:, cols] = r[0:128].astype(BF)
        oth[:, cols] = r[128:256].astype(BF)
        return carry

    lax.fori_loop(0, 4, step, 0)


def combine(mine, got, part, inv, corr_own, corr_got):
    r = inv[:, 0:1]
    c = (corr_own[:, 0:1] + corr_got[:, 0:1]) * (r * (1.0 / 4096))
    h = part[0:128, :].astype(F32)
    g = part[128:136, :].astype(F32)[0:1]
    return r * (g * (mine.astype(F32) + got.astype(F32)) - h * c)


def one_kernel(mine, got, part, inv, corr_own, corr_got, out):
    out[...] = combine(mine[...], got[...], part, inv, corr_own, corr_got).astype(BF)


def two_kernel(mine, got, part_a, part_b, inv, corr_own, corr_got, out_a, out_b):
    out_a[...] = combine(mine[0], got[0], part_a, inv, corr_own, corr_got).astype(BF)
    out_b[...] = combine(mine[1], got[1], part_b, inv, corr_own, corr_got).astype(BF)


def last_kernel(mine, got, part, inv, corr_own, corr_got, cot, r1, r2, r3, out):
    grad = combine(mine[...], got[...], part, inv, corr_own, corr_got)
    grad = grad + r1[...].astype(F32) + r2[...].astype(F32) + r3[...].astype(F32)
    out[...] = (cot[...].astype(F32) + grad).astype(BF)


def gm_kernel(c0, c1, c2, c3, ow, mine, other):
    _, _, core, z = place()
    for ref, which in ((mine, core), (other, 1 - core)):
        rows = pl.ds(pl.multiple_of(which * 256, 256), 256)
        total = jnp.zeros((128, 256), F32)
        for d, c in enumerate((c0, c1, c2, c3)):
            cols = pl.ds(pl.multiple_of(((z + 4 - d) % 4) * 1024, 1024), 1024)
            total = total + dot_nt(c[...], ow[rows, cols])
        ref[...] = total


def out_quarter(mine, got, ow, d):
    _, _, core, z = place()
    cols = pl.ds(pl.multiple_of(((z + d) % 4) * 1024, 1024), 1024)
    rows = pl.ds(pl.multiple_of(core * 256, 256), 256)
    rows_got = pl.ds(pl.multiple_of((1 - core) * 256, 256), 256)
    return dot_nn(mine[...], ow[rows, cols]) + dot_nn(got[...], ow[rows_got, cols])


def out_first_kernel(mine, got, ow, o2):
    o2[...] = out_quarter(mine, got, ow, 2).astype(BF)


def out_rest_kernel(mine, got, ow, o1, o3, o0):
    o1[...] = out_quarter(mine, got, ow, 1).astype(BF)
    o3[...] = out_quarter(mine, got, ow, 3).astype(BF)
    o0[...] = out_quarter(mine, got, ow, 0)


VM = pl.BlockSpec(memory_space=pltpu.VMEM)
AN = pl.BlockSpec(memory_space=pl.ANY)
HB = pl.BlockSpec(memory_space=pltpu.HBM)
PARAMS = pltpu.CompilerParams(vmem_limit_bytes=16 * 1024 * 1024)


def shape(dims, dtype):
    return jax.ShapeDtypeStruct(dims, dtype)


def call(kernel, ins, outs, args, scratch=()):
    return pl.pallas_call(
        kernel,
        in_specs=ins,
        out_specs=[spec for spec, _ in outs],
        out_shape=[sh for _, sh in outs],
        scratch_shapes=list(scratch),
        compiler_params=PARAMS,
    )(*args)


BLOCK = (2, 3, 128, 256)


def in_hbm(value):
    return pltpu.with_memory_space_constraint(value, pltpu.HBM)


def prepare(tokens, position, gain):
    return call(
        prepare_kernel, [HB] * 3, [(VM, shape((136, 1024), BF))],
        (in_hbm(tokens), in_hbm(position), in_hbm(gain)),
        (
            pltpu.VMEM((16, 8, 1024), BF), pltpu.VMEM((16, 1024), BF), pltpu.VMEM((1024,), BF),
            pltpu.SemaphoreType.DMA((3,)),
        ),
    )[0]


def normalise(parts):
    return call(
        norm_kernel, [VM] * 4,
        [(VM, shape((16, 128, 256), BF)), (VM, shape((128, 128), F32))], parts,
    )


WALL = pltpu.HBM((16,) + BLOCK, BF)


def project_early(own, oth, weights):
    return call(
        project_early_kernel, [VM, VM] + [VM] * 9,
        [(VM, shape((256, 768), F32)), (HB, WALL)],
        (own, oth) + weights,
        (pltpu.SemaphoreType.DMA((9,)),),
    )


def project_late(own, oth, acc, wall, weights):
    return pl.pallas_call(
        project_late_kernel,
        in_specs=[VM, VM, VM, HB] + [VM] * 6,
        out_specs=[VM, VM, HB],
        out_shape=[shape((256, 768), BF), shape((16, 2, 16, HD), BF), WALL],
        scratch_shapes=[pltpu.SemaphoreType.DMA((6,))],
        input_output_aliases={3: 2},
        compiler_params=PARAMS,
        name="late",
    )(own, oth, acc, in_hbm(wall), *weights)


def across(proj, agg):
    return call(
        across_kernel, [VM] * 2,
        [(VM, shape((128, 256), BF)), (VM, shape((128, 256), BF)), (VM, shape((2, 256, 256), F32))],
        (proj, agg),
    )


def across_back(proj, agg, gm_mine, gm_got, soft):
    return call(
        across_back_kernel, [VM] * 5,
        [(VM, shape((256, 512), F32)), (VM, shape((16, 2, 16, HD), BF))],
        (proj, agg, gm_mine, gm_got, soft),
    )


def backward(proj, gg, ragg, wall):
    return call(
        back_kernel, [VM] * 3 + [HB],
        [
            (VM, shape((128, 1024), BF)), (VM, shape((128, 1024), BF)), (VM, shape((256, 768), BF)),
            (VM, shape((128, 128), F32)), (VM, shape((128, 128), F32)),
        ],
        (proj, gg, ragg, in_hbm(wall)),
        (pltpu.VMEM((4,) + BLOCK, BF), pltpu.SemaphoreType.DMA((4,))),
    )


def side(stk, wall):
    return call(
        side_kernel, [VM, HB], [(VM, shape((2, 128, 1024), BF))] * 2, (stk, in_hbm(wall)),
        (pltpu.VMEM((8,) + BLOCK, BF), pltpu.SemaphoreType.DMA((8,))),
    )


def home(stk, wall):
    return call(
        home_kernel, [VM, HB], [(VM, shape((128, 1024), BF))] * 2, (stk, in_hbm(wall)),
        (pltpu.VMEM((4,) + BLOCK, BF), pltpu.SemaphoreType.DMA((4,))),
    )


def own_weights(qkv_weight, core):
    mine = lax.dynamic_slice_in_dim(qkv_weight, core * 256, 256, 2)
    other = lax.dynamic_slice_in_dim(qkv_weight, (1 - core) * 256, 256, 2)
    got = swap(other)
    lead = core == 0
    return jnp.stack([jnp.where(lead, mine, got), jnp.where(lead, got, mine)])


def gather_weights(own):
    def near(value, step):
        return lax.ppermute(value, "chan", ring(True, step))

    def cross(value, step):
        return lax.ppermute(value, "chan", ring(False, step))

    r = near(own, 1)
    l = near(own, -1)

    up = cross(own, 1)
    down = cross(own, -1)
    pair = jnp.stack([r, l])
    far = jnp.concatenate([near(r[:1], 1), near(l[1:], -1)], 0)
    pair_up = cross(pair, 1)
    pair_down = cross(pair, -1)
    over_a = cross(up[:1], 1)
    over_b = cross(down[1:], -1)
    far_up = cross(far, 1)
    far_down = cross(far, -1)
    pair_a = cross(pair_up[0], 1)
    pair_b = cross(pair_down[1], -1)
    far_a = cross(far_up[:1], 1)
    far_b = cross(far_down[1:], -1)

    def whole(value):
        return value.reshape((-1,) + value.shape[-4:])

    lead = tuple(whole(v) for v in (own, pair, far, up, down, pair_up, pair_down, far_up, far_down))
    tail = (over_a, over_b, whole(pair_a), whole(pair_b), far_a, far_b)
    return lead, tail, far


def layer(tokens, position, gain, qkv_weight, out_weight, cotangent):
    _, _, core, _ = place()

    own_w = own_weights(qkv_weight, core)
    message = prepare(tokens, position, gain)
    h_parts = [message]
    for d in (1, 2, 3):
        h_parts.append(zshift(message, d))
    early, late, far = gather_weights(own_w)

    waited, _ = lax.optimization_barrier((h_parts, far))
    normed, inv_rms = normalise(waited)
    cot = cotangent.reshape(128, 1024)
    c_parts = [cot]
    for d in (1, 2, 3):
        c_parts.append(zshift(cot, d))
    normed_other = swap(normed)
    acc, wall = project_early(normed, normed_other, early)
    proj, agg, wall = project_late(normed, normed_other, acc, wall, late)
    agg_all = lax.all_to_all(agg, "chan", 0, 0, axis_index_groups=SAME_CORE, tiled=True)

    gm_mine, gm_other = call(
        gm_kernel, [VM] * 5, [(VM, shape((128, 256), F32))] * 2, c_parts + [out_weight],
    )
    gm_got = swap(gm_other)

    mix_own, mix_oth, soft = across(proj, agg_all)
    mix_got = swap(mix_oth)
    gg, gagg = across_back(proj, agg_all, gm_mine, gm_got, soft)
    ragg = lax.all_to_all(gagg, "chan", 0, 0, axis_index_groups=SAME_CORE, tiled=True)

    o2, = call(
        out_first_kernel, [VM] * 3, [(VM, shape((128, 1024), BF))], (mix_own, mix_got, out_weight),
    )
    s2 = zshift(o2, 2)
    o1, o3, o0 = call(
        out_rest_kernel, [VM] * 3,
        [(VM, shape((128, 1024), BF)), (VM, shape((128, 1024), BF)), (VM, shape((128, 1024), F32))],
        (mix_own, mix_got, out_weight),
    )
    s1 = zshift(o1, 1)
    s3 = zshift(o3, 3)
    summed = o0 + s1.astype(F32) + s2.astype(F32) + s3.astype(F32)
    layer_out = (summed + message[:128].astype(F32)).astype(BF)

    own2, oth2, stk, corr_own, corr_oth = backward(proj, gg, ragg, wall)
    got2 = swap(oth2)
    corr_got = swap(corr_oth)
    own_r, oth_r = side(stk, wall)
    got_r = swap(oth_r)
    scal = (inv_rms, corr_own, corr_got)
    msg2, = call(one_kernel, [VM] * 6, [(VM, shape((128, 1024), BF))], (own2, got2, h_parts[2]) + scal)
    r2 = zshift(msg2, 2)
    msg1, msg3 = call(
        two_kernel, [VM] * 7, [(VM, shape((128, 1024), BF))] * 2,
        (own_r, got_r, h_parts[3], h_parts[1]) + scal,
    )
    r1 = zshift(msg1, 1)
    r3 = zshift(msg3, 3)
    own_h, oth_h = home(stk, wall)
    got_h = swap(oth_h)
    input_grad, = call(
        last_kernel, [VM] * 10, [(VM, shape((128, 1024), BF))],
        (own_h, got_h, h_parts[0]) + scal + (cot, r1, r2, r3),
    )
    return layer_out.reshape(16, 8, 1024), input_grad.reshape(16, 8, 1024)


def solution(mesh):
    return jax.shard_map(
        layer,
        mesh=mesh,
        in_specs=(
            P("chan", "region", "head"),
            P("chan", "head"),
            P("head"),
            P(None, "chan", "head"),
            P("head", None),
            P("chan", "region", "head"),
        ),
        out_specs=(P("chan", "region", "head"), P("chan", "region", "head")),
        check_vma=False,
    )
```

profile of v0, /device:TPU:193, one launch (start us, length us, event | category | flops | bytes accessed | tf_op | source)
XLA Modules:
  0.0 172.0 jit_solution(5290770071315196387)
XLA Ops:
  10.7 2.3 %collective-permute-done.4 = bf16[2,3,128,256]{3,2,1,0:T(8,128)(2,1)S(1)} collective-permute-done((bf16[2,3,128,256]{3,2,1,0:T(8,128)(2,1)S(1)}, bf16[2,3,128,256]{3,2,1,0:T(8,128)(2,1)S(1)}, u32[]{:S(2)}, u32[]{:S(2)}) %collective-permute-start.4) | collective-permute-done | bytes 393248 | tf_op jit(solution)/shard_map/ppermute | solution.py:539
  18.0 10.9 %collective-permute-done.1.p2.part = bf16[136,1024]{1,0:T(8,128)(2,1)S(1)} collective-permute-done((bf16[136,1024]{1,0:T(8,128)(2,1)S(1)}, bf16[136,1024]{1,0:T(8,128)(2,1)S(1)}, u32[]{:S(2)}, u32[]{:S(2)}) %collective-permute-start.1) | collective-permute-done | bytes 278560 | tf_op jit(solution)/shard_map/ppermute | solution.py:42
  30.2 4.6 %collective-permute-done.2.p3.part_a = bf16[136,1024]{1,0:T(8,128)(2,1)S(1)} collective-permute-done((bf16[136,1024]{1,0:T(8,128)(2,1)S(1)}, bf16[136,1024]{1,0:T(8,128)(2,1)S(1)}, u32[]{:S(2)}, u32[]{:S(2)}) %collective-permute-start.2) | collective-permute-done | bytes 278560 | tf_op jit(solution)/shard_map/ppermute | solution.py:42
  36.2 2.5 %collective-permute-start.10 = (bf16[2,3,128,256]{3,2,1,0:T(8,128)(2,1)S(1)}, bf16[2,3,128,256]{3,2,1,0:T(8,128)(2,1)S(1)}, u32[]{:S(2)}, u32[]{:S(2)}) collective-permute-start(bf16[2,3,128,256]{3,2,1,0:T(8,128)(2,1)S(1)} %get-tuple-element.69), channel_id=1, source_target_pairs={{0,192},{8,56},{16,208},{24,8},{32,224},{40,24},{48,240},{56,40},{... | collective-permute-start | bytes 1179656 | tf_op jit(solution)/shard_map/ppermute | solution.py:542
  39.7 2.7 %collective-permute-start.25 = (bf16[128,1024]{1,0:T(8,128)(2,1)}, bf16[128,1024]{1,0:T(8,128)(2,1)S(1)}, u32[]{:S(2)}, u32[]{:S(2)}) collective-permute-start(bf16[128,1024]{1,0:T(8,128)(2,1)} %bitcast.23), channel_id=1, source_target_pairs={{0,2},{2,4},{4,6},{6,0},{1,3},{3,5},{5,7},{7,1},{8,10},{10,12},{12... | collective-permute-start | bytes 786440 | tf_op jit(solution)/shard_map/ppermute | solution.py:42
  42.9 3.3 %collective-permute-start.8 = (bf16[16,128,256]{2,1,0:T(8,128)(2,1)S(1)}, bf16[16,128,256]{2,1,0:T(8,128)(2,1)S(1)}, u32[]{:S(2)}, u32[]{:S(2)}) collective-permute-start(bf16[16,128,256]{2,1,0:T(8,128)(2,1)S(1)} %get-tuple-element.38.own), channel_id=1, source_target_pairs={{0,8},{8,0},{16,24},{24,16},{32,40},{40,32},{48,56},{56,48},{64,72... | collective-permute-start | bytes 3145736 | tf_op jit(solution)/shard_map/ppermute | solution.py:38
  51.6 8.3 %collective-permute-done.26.c2 = bf16[128,1024]{1,0:T(8,128)(2,1)S(1)} collective-permute-done((bf16[128,1024]{1,0:T(8,128)(2,1)S(1)}, bf16[128,1024]{1,0:T(8,128)(2,1)S(1)}, u32[]{:S(2)}, u32[]{:S(2)}) %collective-permute-start.26) | collective-permute-done | bytes 262176 | tf_op jit(solution)/shard_map/ppermute | solution.py:42
  60.0 2.3 %collective-permute-start.15 = (bf16[1,3,128,256]{3,2,1,0:T(8,128)(2,1)S(1)}, bf16[1,3,128,256]{3,2,1,0:T(8,128)(2,1)S(1)}, u32[]{:S(2)}, u32[]{:S(2)}) collective-permute-start(bf16[1,3,128,256]{3,2,1,0:T(8,128)(2,1)S(1)} %slice.38), channel_id=1, source_target_pairs={{0,64},{8,24},{16,80},{24,40},{32,96},{40,56},{48,112},{56,8},{64,... | collective-permute-start | bytes 589832 | tf_op jit(solution)/shard_map/ppermute | solution.py:542
  62.3 3.3 %collective-permute-done.27.c3 = bf16[128,1024]{1,0:T(8,128)(2,1)S(1)} collective-permute-done((bf16[128,1024]{1,0:T(8,128)(2,1)S(1)}, bf16[128,1024]{1,0:T(8,128)(2,1)S(1)}, u32[]{:S(2)}, u32[]{:S(2)}) %collective-permute-start.27) | collective-permute-done | bytes 262176 | tf_op jit(solution)/shard_map/ppermute | solution.py:42
  65.6 3.4 %collective-permute-start.16 = (bf16[1,3,128,256]{3,2,1,0:T(8,128)(2,1)S(1)}, bf16[1,3,128,256]{3,2,1,0:T(8,128)(2,1)S(1)}, u32[]{:S(2)}, u32[]{:S(2)}) collective-permute-start(bf16[1,3,128,256]{3,2,1,0:T(8,128)(2,1)S(1)} %slice.39), channel_id=1, source_target_pairs={{0,192},{8,56},{16,208},{24,8},{32,224},{40,24},{48,240},{56,40},{... | collective-permute-start | bytes 589832 | tf_op jit(solution)/shard_map/ppermute | solution.py:542
  69.0 2.7 %collective-permute-start.18 = (bf16[2,3,128,256]{3,2,1,0:T(8,128)(2,1)S(1)}, bf16[2,3,128,256]{3,2,1,0:T(8,128)(2,1)S(1)}, u32[]{:S(2)}, u32[]{:S(2)}) collective-permute-start(bf16[2,3,128,256]{3,2,1,0:T(8,128)(2,1)S(1)} %slice_bitcast_fusion), channel_id=1, source_target_pairs={{0,192},{8,56},{16,208},{24,8},{32,224},{40,24},{48,240},{56,40},{... | collective-permute-start | bytes 1179656 | tf_op jit(solution)/shard_map/ppermute | solution.py:542
  71.8 2.9 %collective-permute-start.20 = (bf16[1,3,128,256]{3,2,1,0:T(8,128)(2,1)S(1)}, bf16[1,3,128,256]{3,2,1,0:T(8,128)(2,1)S(1)}, u32[]{:S(2)}, u32[]{:S(2)}) collective-permute-start(bf16[1,3,128,256]{3,2,1,0:T(8,128)(2,1)S(1)} %slice.43), channel_id=1, source_target_pairs={{0,192},{8,56},{16,208},{24,8},{32,224},{40,24},{48,240},{56,40},{... | collective-permute-start | bytes 589832 | tf_op jit(solution)/shard_map/ppermute | solution.py:542
  77.3 3.3 %shard_map.79 = (f32[256,768]{1,0:T(8,128)S(1)}, bf16[16,2,3,128,256]{4,3,2,1,0:T(8,128)(2,1)}) custom-call(bf16[16,128,256]{2,1,0:T(8,128)(2,1)S(1)} %get-tuple-element.38.own, bf16[16,128,256]{2,1,0:T(8,128)(2,1)S(1)} %collective-permute-done.8.oth, bf16[1,2,3,128,256]{4,3,2,1,0:T(8,128)(2,1)S(1)} %get-tuple-element.68.refs_0_, ...), custom_call_target="tpu_custom_call" | custom-call | tf_op jit(solution)/shard_map/pallas_call | solution.py:427
  82.7 13.6 %all_to_all.10.agg = bf16[16,2,16,128]{3,2,1,0:T(8,128)(2,1)S(1)} all-to-all(bf16[16,2,16,128]{3,2,1,0:T(8,128)(2,1)S(1)} %get-tuple-element.42), channel_id=1, replica_groups={{0,16,32,48,64,80,96,112,128,144,160,176,192,208,224,240},{8,24,40,56,7..., dimensions={0} | all-to-all | bytes 262144 | tf_op jit(solution)/shard_map/all_to_all | solution.py:589
  98.4 9.9 %all_to_all.11.ragg = bf16[16,2,16,128]{3,2,1,0:T(8,128)(2,1)S(1)} all-to-all(bf16[16,2,16,128]{3,2,1,0:T(8,128)(2,1)S(1)} %get-tuple-element.52), channel_id=1, replica_groups={{0,16,32,48,64,80,96,112,128,144,160,176,192,208,224,240},{8,24,40,56,7..., dimensions={0} | all-to-all | bytes 262144 | tf_op jit(solution)/shard_map/all_to_all | solution.py:599
  108.3 3.6 %shard_map.85 = (bf16[128,1024]{1,0:T(8,128)(2,1)S(1)}, bf16[128,1024]{1,0:T(8,128)(2,1)S(1)}, bf16[256,768]{1,0:T(8,128)(2,1)S(1)}, f32[128,128]{1,0:T(8,128)S(1)}, f32[128,128]{1,0:T(8,128)S(1)}) custom-call(bf16[256,768]{1,0:T(8,128)(2,1)S(1)} %get-tuple-element.41.proj, f32[256,512]{1,0:T(8,128)S(1)} %get-tuple-element.51.gg, ...), custom_call_target="tpu_custom_call" | custom-call | tf_op jit(solution)/shard_map/pallas_call | solution.py:427
  112.0 3.9 %shard_map.87 = (bf16[2,128,1024]{2,1,0:T(8,128)(2,1)S(1)}, bf16[2,128,1024]{2,1,0:T(8,128)(2,1)S(1)}) custom-call(bf16[256,768]{1,0:T(8,128)(2,1)S(1)} %get-tuple-element.54.stk, bf16[16,2,3,128,256]{4,3,2,1,0:T(8,128)(2,1)} %get-tuple-element.53.wall), custom_call_target="tpu_custom_call" | custom-call | tf_op jit(solution)/shard_map/pallas_call | solution.py:427
  115.9 4.6 %collective-permute-start.31 = (bf16[2,128,1024]{2,1,0:T(8,128)(2,1)S(1)}, bf16[2,128,1024]{2,1,0:T(8,128)(2,1)S(1)}, u32[]{:S(2)}, u32[]{:S(2)}) collective-permute-start(bf16[2,128,1024]{2,1,0:T(8,128)(2,1)S(1)} %get-tuple-element.61), channel_id=1, source_target_pairs={{0,8},{8,0},{16,24},{24,16},{32,40},{40,32},{48,56},{56,48},{64,72... | collective-permute-start | bytes 1572872 | tf_op jit(solution)/shard_map/ppermute | solution.py:38
  125.6 2.6 %shard_map.86 = (bf16[128,1024]{1,0:T(8,128)(2,1)S(1)}, bf16[128,1024]{1,0:T(8,128)(2,1)S(1)}) custom-call(bf16[256,768]{1,0:T(8,128)(2,1)S(1)} %get-tuple-element.54.stk, bf16[16,2,3,128,256]{4,3,2,1,0:T(8,128)(2,1)} %get-tuple-element.53.wall), custom_call_target="tpu_custom_call" | custom-call | tf_op jit(solution)/shard_map/pallas_call | solution.py:427
  129.5 3.5 %collective-permute-start.34 = (bf16[128,1024]{1,0:T(8,128)(2,1)S(1)}, bf16[128,1024]{1,0:T(8,128)(2,1)S(1)}, u32[]{:S(2)}, u32[]{:S(2)}) collective-permute-start(bf16[128,1024]{1,0:T(8,128)(2,1)S(1)} %shard_map.89), channel_id=1, source_target_pairs={{0,4},{2,6},{4,0},{6,2},{1,5},{3,7},{5,1},{7,3},{8,12},{10,14},{12... | collective-permute-start | bytes 786440 | tf_op jit(solution)/shard_map/ppermute | solution.py:42
  133.3 6.0 %collective-permute-done.23 = bf16[128,1024]{1,0:T(8,128)(2,1)S(1)} collective-permute-done((bf16[128,1024]{1,0:T(8,128)(2,1)S(1)}, bf16[128,1024]{1,0:T(8,128)(2,1)S(1)}, u32[]{:S(2)}, u32[]{:S(2)}) %collective-permute-start.23) | collective-permute-done | bytes 262176 | tf_op jit(solution)/shard_map/ppermute | solution.py:42
  139.3 15.4 %collective-permute-done.22 = bf16[128,1024]{1,0:T(8,128)(2,1)S(1)} collective-permute-done((bf16[128,1024]{1,0:T(8,128)(2,1)S(1)}, bf16[128,1024]{1,0:T(8,128)(2,1)S(1)}, u32[]{:S(2)}, u32[]{:S(2)}) %collective-permute-start.22) | collective-permute-done | bytes 262176 | tf_op jit(solution)/shard_map/ppermute | solution.py:42
  157.1 4.8 %collective-permute-done.34.r2 = bf16[128,1024]{1,0:T(8,128)(2,1)S(1)} collective-permute-done((bf16[128,1024]{1,0:T(8,128)(2,1)S(1)}, bf16[128,1024]{1,0:T(8,128)(2,1)S(1)}, u32[]{:S(2)}, u32[]{:S(2)}) %collective-permute-start.34) | collective-permute-done | bytes 262176 | tf_op jit(solution)/shard_map/ppermute | solution.py:42
  161.8 9.1 %collective-permute-done.32.r1 = bf16[128,1024]{1,0:T(8,128)(2,1)S(1)} collective-permute-done((bf16[128,1024]{1,0:T(8,128)(2,1)S(1)}, bf16[128,1024]{1,0:T(8,128)(2,1)S(1)}, u32[]{:S(2)}, u32[]{:S(2)}) %collective-permute-start.32) | collective-permute-done | bytes 262176 | tf_op jit(solution)/shard_map/ppermute | solution.py:42
  (84 shorter events, 41.5 us)
Async XLA Ops:
  9.5 19.4 %collective-permute-start.1 = (bf16[136,1024]{1,0:T(8,128)(2,1)S(1)}, bf16[136,1024]{1,0:T(8,128)(2,1)S(1)}, u32[]{:S(2)}, u32[]{:S(2)}) collective-permute-start(bf16[136,1024]{1,0:T(8,128)(2,1)S(1)} %shard_map.77.p0.part), channel_id=1, source_target_pairs={{0,4},{2,6},{4,0},{6,2},{1,5},{3,7},{5,1},{7,3},{8,12},{10,14},{12... | collective-permute-start | bytes 835592 | tf_op jit(solution)/shard_map/ppermute | solution.py:42
  13.1 35.1 %collective-permute-start.11 = (bf16[2,2,3,128,256]{4,3,2,1,0:T(8,128)(2,1)S(1)}, bf16[2,2,3,128,256]{4,3,2,1,0:T(8,128)(2,1)S(1)}, u32[]{:S(2)}, u32[]{:S(2)}) collective-permute-start(bf16[2,2,3,128,256]{4,3,2,1,0:T(8,128)(2,1)S(1)} %pad_maximum_fusion.refs_1_), channel_id=1, source_target_pairs={{0,64},{8,24},{16,80},{24,40},{32,96},{40,56},{48,112},{56,8},{64,... | collective-permute-start | bytes 2359304 | tf_op jit(solution)/shard_map/ppermute | solution.py:542
  14.4 35.7 %collective-permute-start.12 = (bf16[2,2,3,128,256]{4,3,2,1,0:T(8,128)(2,1)S(1)}, bf16[2,2,3,128,256]{4,3,2,1,0:T(8,128)(2,1)S(1)}, u32[]{:S(2)}, u32[]{:S(2)}) collective-permute-start(bf16[2,2,3,128,256]{4,3,2,1,0:T(8,128)(2,1)S(1)} %pad_maximum_fusion.refs_1_), channel_id=1, source_target_pairs={{0,192},{8,56},{16,208},{24,8},{32,224},{40,24},{48,240},{56,40},{... | collective-permute-start | bytes 2359304 | tf_op jit(solution)/shard_map/ppermute | solution.py:542
  15.9 19.0 %collective-permute-start.2 = (bf16[136,1024]{1,0:T(8,128)(2,1)S(1)}, bf16[136,1024]{1,0:T(8,128)(2,1)S(1)}, u32[]{:S(2)}, u32[]{:S(2)}) collective-permute-start(bf16[136,1024]{1,0:T(8,128)(2,1)S(1)} %shard_map.77.p0.part), channel_id=1, source_target_pairs={{0,6},{2,0},{4,2},{6,4},{1,7},{3,1},{5,3},{7,5},{8,14},{10,8},{12,... | collective-permute-start | bytes 835592 | tf_op jit(solution)/shard_map/ppermute | solution.py:42
  16.6 19.6 %collective-permute-start.5 = (bf16[1,3,128,256]{3,2,1,0:T(8,128)(2,1)S(1)}, bf16[1,3,128,256]{3,2,1,0:T(8,128)(2,1)S(1)}, u32[]{:S(2)}, u32[]{:S(2)}) collective-permute-start(bf16[1,3,128,256]{3,2,1,0:T(8,128)(2,1)S(1)} %slice.36), channel_id=1, source_target_pairs={{0,16},{8,72},{16,32},{24,88},{32,48},{40,104},{48,0},{56,120},{64... | collective-permute-start | bytes 589832 | tf_op jit(solution)/shard_map/ppermute | solution.py:539
  28.9 14.0 %collective-permute-start.9 = (bf16[2,3,128,256]{3,2,1,0:T(8,128)(2,1)S(1)}, bf16[2,3,128,256]{3,2,1,0:T(8,128)(2,1)S(1)}, u32[]{:S(2)}, u32[]{:S(2)}) collective-permute-start(bf16[2,3,128,256]{3,2,1,0:T(8,128)(2,1)S(1)} %get-tuple-element.69), channel_id=1, source_target_pairs={{0,64},{8,24},{16,80},{24,40},{32,96},{40,56},{48,112},{56,8},{64,... | collective-permute-start | bytes 1179656 | tf_op jit(solution)/shard_map/ppermute | solution.py:542
  36.2 10.0 %collective-permute-start.10 = (bf16[2,3,128,256]{3,2,1,0:T(8,128)(2,1)S(1)}, bf16[2,3,128,256]{3,2,1,0:T(8,128)(2,1)S(1)}, u32[]{:S(2)}, u32[]{:S(2)}) collective-permute-start(bf16[2,3,128,256]{3,2,1,0:T(8,128)(2,1)S(1)} %get-tuple-element.69), channel_id=1, source_target_pairs={{0,192},{8,56},{16,208},{24,8},{32,224},{40,24},{48,240},{56,40},{... | collective-permute-start | bytes 1179656 | tf_op jit(solution)/shard_map/ppermute | solution.py:542
  42.9 33.4 %collective-permute-start.8 = (bf16[16,128,256]{2,1,0:T(8,128)(2,1)S(1)}, bf16[16,128,256]{2,1,0:T(8,128)(2,1)S(1)}, u32[]{:S(2)}, u32[]{:S(2)}) collective-permute-start(bf16[16,128,256]{2,1,0:T(8,128)(2,1)S(1)} %get-tuple-element.38.own), channel_id=1, source_target_pairs={{0,8},{8,0},{16,24},{24,16},{32,40},{40,32},{48,56},{56,48},{64,72... | collective-permute-start | bytes 3145736 | tf_op jit(solution)/shard_map/ppermute | solution.py:38
  46.3 13.7 %collective-permute-start.26 = (bf16[128,1024]{1,0:T(8,128)(2,1)S(1)}, bf16[128,1024]{1,0:T(8,128)(2,1)S(1)}, u32[]{:S(2)}, u32[]{:S(2)}) collective-permute-start(bf16[128,1024]{1,0:T(8,128)(2,1)S(1)} %bitcast.24), channel_id=1, source_target_pairs={{0,4},{2,6},{4,0},{6,2},{1,5},{3,7},{5,1},{7,3},{8,12},{10,14},{12... | collective-permute-start | bytes 786440 | tf_op jit(solution)/shard_map/ppermute | solution.py:42
  47.7 17.9 %collective-permute-start.27 = (bf16[128,1024]{1,0:T(8,128)(2,1)S(1)}, bf16[128,1024]{1,0:T(8,128)(2,1)S(1)}, u32[]{:S(2)}, u32[]{:S(2)}) collective-permute-start(bf16[128,1024]{1,0:T(8,128)(2,1)S(1)} %bitcast.25), channel_id=1, source_target_pairs={{0,6},{2,0},{4,2},{6,4},{1,7},{3,1},{5,3},{7,5},{8,14},{10,8},{12,... | collective-permute-start | bytes 786440 | tf_op jit(solution)/shard_map/ppermute | solution.py:42
  48.2 20.8 %collective-permute-start.13 = (bf16[2,3,128,256]{3,2,1,0:T(8,128)(2,1)S(1)}, bf16[2,3,128,256]{3,2,1,0:T(8,128)(2,1)S(1)}, u32[]{:S(2)}, u32[]{:S(2)}) collective-permute-start(bf16[2,3,128,256]{3,2,1,0:T(8,128)(2,1)S(1)} %constant_dynamic-update-slice_fusion), channel_id=1, source_target_pairs={{0,64},{8,24},{16,80},{24,40},{32,96},{40,56},{48,112},{56,8},{64,... | collective-permute-start | bytes 1179656 | tf_op jit(solution)/shard_map/ppermute | solution.py:542
  50.0 19.0 %collective-permute-start.14 = (bf16[2,3,128,256]{3,2,1,0:T(8,128)(2,1)S(1)}, bf16[2,3,128,256]{3,2,1,0:T(8,128)(2,1)S(1)}, u32[]{:S(2)}, u32[]{:S(2)}) collective-permute-start(bf16[2,3,128,256]{3,2,1,0:T(8,128)(2,1)S(1)} %constant_dynamic-update-slice_fusion), channel_id=1, source_target_pairs={{0,192},{8,56},{16,208},{24,8},{32,224},{40,24},{48,240},{56,40},{... | collective-permute-start | bytes 1179656 | tf_op jit(solution)/shard_map/ppermute | solution.py:542
  60.0 11.8 %collective-permute-start.15 = (bf16[1,3,128,256]{3,2,1,0:T(8,128)(2,1)S(1)}, bf16[1,3,128,256]{3,2,1,0:T(8,128)(2,1)S(1)}, u32[]{:S(2)}, u32[]{:S(2)}) collective-permute-start(bf16[1,3,128,256]{3,2,1,0:T(8,128)(2,1)S(1)} %slice.38), channel_id=1, source_target_pairs={{0,64},{8,24},{16,80},{24,40},{32,96},{40,56},{48,112},{56,8},{64,... | collective-permute-start | bytes 589832 | tf_op jit(solution)/shard_map/ppermute | solution.py:542
  69.0 11.6 %collective-permute-start.17 = (bf16[2,3,128,256]{3,2,1,0:T(8,128)(2,1)S(1)}, bf16[2,3,128,256]{3,2,1,0:T(8,128)(2,1)S(1)}, u32[]{:S(2)}, u32[]{:S(2)}) collective-permute-start(bf16[2,3,128,256]{3,2,1,0:T(8,128)(2,1)S(1)} %slice_bitcast_fusion.1), channel_id=1, source_target_pairs={{0,64},{8,24},{16,80},{24,40},{32,96},{40,56},{48,112},{56,8},{64,... | collective-permute-start | bytes 1179656 | tf_op jit(solution)/shard_map/ppermute | solution.py:542
  69.0 11.6 %collective-permute-start.18 = (bf16[2,3,128,256]{3,2,1,0:T(8,128)(2,1)S(1)}, bf16[2,3,128,256]{3,2,1,0:T(8,128)(2,1)S(1)}, u32[]{:S(2)}, u32[]{:S(2)}) collective-permute-start(bf16[2,3,128,256]{3,2,1,0:T(8,128)(2,1)S(1)} %slice_bitcast_fusion), channel_id=1, source_target_pairs={{0,192},{8,56},{16,208},{24,8},{32,224},{40,24},{48,240},{56,40},{... | collective-permute-start | bytes 1179656 | tf_op jit(solution)/shard_map/ppermute | solution.py:542
  76.3 21.1 %collective-permute-start.28 = (f32[128,256]{1,0:T(8,128)S(1)}, f32[128,256]{1,0:T(8,128)S(1)}, u32[]{:S(2)}, u32[]{:S(2)}) collective-permute-start(f32[128,256]{1,0:T(8,128)S(1)} %get-tuple-element.49), channel_id=1, source_target_pairs={{0,8},{8,0},{16,24},{24,16},{32,40},{40,32},{48,56},{56,48},{64,72... | collective-permute-start | bytes 393224 | tf_op jit(solution)/shard_map/ppermute | solution.py:38
  115.9 13.6 %collective-permute-start.31 = (bf16[2,128,1024]{2,1,0:T(8,128)(2,1)S(1)}, bf16[2,128,1024]{2,1,0:T(8,128)(2,1)S(1)}, u32[]{:S(2)}, u32[]{:S(2)}) collective-permute-start(bf16[2,128,1024]{2,1,0:T(8,128)(2,1)S(1)} %get-tuple-element.61), channel_id=1, source_target_pairs={{0,8},{8,0},{16,24},{24,16},{32,40},{40,32},{48,56},{56,48},{64,72... | collective-permute-start | bytes 1572872 | tf_op jit(solution)/shard_map/ppermute | solution.py:38
  122.4 16.9 %collective-permute-start.23 = (bf16[128,1024]{1,0:T(8,128)(2,1)S(1)}, bf16[128,1024]{1,0:T(8,128)(2,1)S(1)}, u32[]{:S(2)}, u32[]{:S(2)}) collective-permute-start(bf16[128,1024]{1,0:T(8,128)(2,1)S(1)} %shard_map.82), channel_id=1, source_target_pairs={{0,4},{2,6},{4,0},{6,2},{1,5},{3,7},{5,1},{7,3},{8,12},{10,14},{12... | collective-permute-start | bytes 786440 | tf_op jit(solution)/shard_map/ppermute | solution.py:42
  123.1 31.7 %collective-permute-start.22 = (bf16[128,1024]{1,0:T(8,128)(2,1)S(1)}, bf16[128,1024]{1,0:T(8,128)(2,1)S(1)}, u32[]{:S(2)}, u32[]{:S(2)}) collective-permute-start(bf16[128,1024]{1,0:T(8,128)(2,1)S(1)} %get-tuple-element.46), channel_id=1, source_target_pairs={{0,2},{2,4},{4,6},{6,0},{1,3},{3,5},{5,7},{7,1},{8,10},{10,12},{12... | collective-permute-start | bytes 786440 | tf_op jit(solution)/shard_map/ppermute | solution.py:42
  124.4 31.8 %collective-permute-start.24 = (bf16[128,1024]{1,0:T(8,128)(2,1)S(1)}, bf16[128,1024]{1,0:T(8,128)(2,1)S(1)}, u32[]{:S(2)}, u32[]{:S(2)}) collective-permute-start(bf16[128,1024]{1,0:T(8,128)(2,1)S(1)} %get-tuple-element.47), channel_id=1, source_target_pairs={{0,6},{2,0},{4,2},{6,4},{1,7},{3,1},{5,3},{7,5},{8,14},{10,8},{12,... | collective-permute-start | bytes 786440 | tf_op jit(solution)/shard_map/ppermute | solution.py:42
  128.2 28.8 %collective-permute-start.29 = (bf16[128,1024]{1,0:T(8,128)(2,1)S(1)}, bf16[128,1024]{1,0:T(8,128)(2,1)S(1)}, u32[]{:S(2)}, u32[]{:S(2)}) collective-permute-start(bf16[128,1024]{1,0:T(8,128)(2,1)S(1)} %get-tuple-element.56), channel_id=1, source_target_pairs={{0,8},{8,0},{16,24},{24,16},{32,40},{40,32},{48,56},{56,48},{64,72... | collective-permute-start | bytes 786440 | tf_op jit(solution)/shard_map/ppermute | solution.py:38
  129.5 32.4 %collective-permute-start.34 = (bf16[128,1024]{1,0:T(8,128)(2,1)S(1)}, bf16[128,1024]{1,0:T(8,128)(2,1)S(1)}, u32[]{:S(2)}, u32[]{:S(2)}) collective-permute-start(bf16[128,1024]{1,0:T(8,128)(2,1)S(1)} %shard_map.89), channel_id=1, source_target_pairs={{0,4},{2,6},{4,0},{6,2},{1,5},{3,7},{5,1},{7,3},{8,12},{10,14},{12... | collective-permute-start | bytes 786440 | tf_op jit(solution)/shard_map/ppermute | solution.py:42
  139.3 31.6 %collective-permute-start.32 = (bf16[128,1024]{1,0:T(8,128)(2,1)S(1)}, bf16[128,1024]{1,0:T(8,128)(2,1)S(1)}, u32[]{:S(2)}, u32[]{:S(2)}) collective-permute-start(bf16[128,1024]{1,0:T(8,128)(2,1)S(1)} %get-tuple-element.62), channel_id=1, source_target_pairs={{0,2},{2,4},{4,6},{6,0},{1,3},{3,5},{5,7},{7,1},{8,10},{10,12},{12... | collective-permute-start | bytes 786440 | tf_op jit(solution)/shard_map/ppermute | solution.py:42
  154.8 16.2 %collective-permute-start.35 = (bf16[128,1024]{1,0:T(8,128)(2,1)S(1)}, bf16[128,1024]{1,0:T(8,128)(2,1)S(1)}, u32[]{:S(2)}, u32[]{:S(2)}) collective-permute-start(bf16[128,1024]{1,0:T(8,128)(2,1)S(1)} %get-tuple-element.65), channel_id=1, source_target_pairs={{0,6},{2,0},{4,2},{6,4},{1,7},{3,1},{5,3},{7,5},{8,14},{10,8},{12,... | collective-permute-start | bytes 786440 | tf_op jit(solution)/shard_map/ppermute | solution.py:42
  (14 other events, 192.4 us)
where the time goes:
time: 172 us
  waiting for transfers between devices  69.3 us (40%)
  starting transfers between devices  51.7 us (30%)
  blocking collectives  23.5 us (14%)
  Pallas kernels  23.1 us (13%)
  other arithmetic  2.21 us (1%)
    ppermute x12, waiting for transfers between devices, zshift(): lax.ppermute(value, 'head', [(i, (i + step) % NZ) for i in range(NZ)])  63.9 us
    ppermute x12, starting transfers between devices, cross(): return lax.ppermute(value, 'chan', ring(False, step))  21.3 us
    pallas_call x14, Pallas kernels, call(): pl.pallas_call(kernel, in_specs=ins, out_specs=[spec for spec, _ in outs]...  21.1 us
    all_to_all x1, blocking collectives, layer(): lax.all_to_all(agg, 'chan', 0, 0, axis_index_groups=SAME_CORE, tiled=True)  13.6 us
    ppermute x12, starting transfers between devices, zshift(): lax.ppermute(value, 'head', [(i, (i + step) % NZ) for i in range(NZ)])  13.5 us
    ppermute x8, starting transfers between devices, swap(): return lax.ppermute(value, 'chan', SWAP)  11.3 us
    all_to_all x1, blocking collectives, layer(): lax.all_to_all(gagg, 'chan', 0, 0, axis_index_groups=SAME_CORE, tiled=True)  9.88 us
    ppermute x4, starting transfers between devices, near(): return lax.ppermute(value, 'chan', ring(True, step))  5.65 us
  transfers between devices with their start and end apart: 36, of which 13 were waited for; matrix products, arithmetic and copies ran while one was open for 1% of the time, Pallas kernels for 8%

commit v1 on v0

--- a/solution.py
+++ b/solution.py
@@ -556,8 +556,10 @@
     far_down = cross(far, -1)
     pair_a = cross(pair_up[0], 1)
     pair_b = cross(pair_down[1], -1)
-    far_a = cross(far_up[:1], 1)
-    far_b = cross(far_down[1:], -1)
+    far_up_half = far_up[:1]
+    far_down_half = far_down[1:]
+    far_a = cross(far_up_half, 1)
+    far_b = cross(far_down_half, -1)
 
     def whole(value):
         return value.reshape((-1,) + value.shape[-4:])

time: 172 us -> 172 us (level)
  no operation moved by 1% of the time
where the time goes in v1:
time: 172 us
  waiting for transfers between devices  69.3 us (40%)
  starting transfers between devices  51.7 us (30%)
  blocking collectives  23.5 us (14%)
  Pallas kernels  23.1 us (13%)
  other arithmetic  2.21 us (1%)
    ppermute x12, waiting for transfers between devices, zshift(): lax.ppermute(value, 'head', [(i, (i + step) % NZ) for i in range(NZ)])  63.9 us
    ppermute x12, starting transfers between devices, cross(): return lax.ppermute(value, 'chan', ring(False, step))  21.3 us
    pallas_call x14, Pallas kernels, call(): pl.pallas_call(kernel, in_specs=ins, out_specs=[spec for spec, _ in outs]...  21.1 us
    all_to_all x1, blocking collectives, layer(): lax.all_to_all(agg, 'chan', 0, 0, axis_index_groups=SAME_CORE, tiled=True)  13.6 us
    ppermute x12, starting transfers between devices, zshift(): lax.ppermute(value, 'head', [(i, (i + step) % NZ) for i in range(NZ)])  13.5 us
    ppermute x8, starting transfers between devices, swap(): return lax.ppermute(value, 'chan', SWAP)  11.3 us
    all_to_all x1, blocking collectives, layer(): lax.all_to_all(gagg, 'chan', 0, 0, axis_index_groups=SAME_CORE, tiled=True)  9.88 us
    ppermute x4, starting transfers between devices, near(): return lax.ppermute(value, 'chan', ring(True, step))  5.65 us
  transfers between devices with their start and end apart: 36, of which 13 were waited for; matrix products, arithmetic and copies ran while one was open for 1% of the time, Pallas kernels for 8%

profile of v1, /device:TPU:193, one launch (start us, length us, event | category | flops | bytes accessed | tf_op | source)
XLA Modules:
  0.0 172.0 jit_solution(5290770071315196387)
XLA Ops:
  10.7 2.3 %collective-permute-done.4 = bf16[2,3,128,256]{3,2,1,0:T(8,128)(2,1)S(1)} collective-permute-done((bf16[2,3,128,256]{3,2,1,0:T(8,128)(2,1)S(1)}, bf16[2,3,128,256]{3,2,1,0:T(8,128)(2,1)S(1)}, u32[]{:S(2)}, u32[]{:S(2)}) %collective-permute-start.4) | collective-permute-done | bytes 393248 | tf_op jit(solution)/shard_map/ppermute | solution.py:539
  18.0 10.9 %collective-permute-done.1.p2.part = bf16[136,1024]{1,0:T(8,128)(2,1)S(1)} collective-permute-done((bf16[136,1024]{1,0:T(8,128)(2,1)S(1)}, bf16[136,1024]{1,0:T(8,128)(2,1)S(1)}, u32[]{:S(2)}, u32[]{:S(2)}) %collective-permute-start.1) | collective-permute-done | bytes 278560 | tf_op jit(solution)/shard_map/ppermute | solution.py:42
  30.2 4.6 %collective-permute-done.2.p3.part_a = bf16[136,1024]{1,0:T(8,128)(2,1)S(1)} collective-permute-done((bf16[136,1024]{1,0:T(8,128)(2,1)S(1)}, bf16[136,1024]{1,0:T(8,128)(2,1)S(1)}, u32[]{:S(2)}, u32[]{:S(2)}) %collective-permute-start.2) | collective-permute-done | bytes 278560 | tf_op jit(solution)/shard_map/ppermute | solution.py:42
  36.2 2.5 %collective-permute-start.10 = (bf16[2,3,128,256]{3,2,1,0:T(8,128)(2,1)S(1)}, bf16[2,3,128,256]{3,2,1,0:T(8,128)(2,1)S(1)}, u32[]{:S(2)}, u32[]{:S(2)}) collective-permute-start(bf16[2,3,128,256]{3,2,1,0:T(8,128)(2,1)S(1)} %get-tuple-element.69), channel_id=1, source_target_pairs={{0,192},{8,56},{16,208},{24,8},{32,224},{40,24},{48,240},{56,40},{... | collective-permute-start | bytes 1179656 | tf_op jit(solution)/shard_map/ppermute | solution.py:542
  39.7 2.7 %collective-permute-start.25 = (bf16[128,1024]{1,0:T(8,128)(2,1)}, bf16[128,1024]{1,0:T(8,128)(2,1)S(1)}, u32[]{:S(2)}, u32[]{:S(2)}) collective-permute-start(bf16[128,1024]{1,0:T(8,128)(2,1)} %bitcast.23), channel_id=1, source_target_pairs={{0,2},{2,4},{4,6},{6,0},{1,3},{3,5},{5,7},{7,1},{8,10},{10,12},{12... | collective-permute-start | bytes 786440 | tf_op jit(solution)/shard_map/ppermute | solution.py:42
  42.9 3.3 %collective-permute-start.8 = (bf16[16,128,256]{2,1,0:T(8,128)(2,1)S(1)}, bf16[16,128,256]{2,1,0:T(8,128)(2,1)S(1)}, u32[]{:S(2)}, u32[]{:S(2)}) collective-permute-start(bf16[16,128,256]{2,1,0:T(8,128)(2,1)S(1)} %get-tuple-element.38.own), channel_id=1, source_target_pairs={{0,8},{8,0},{16,24},{24,16},{32,40},{40,32},{48,56},{56,48},{64,72... | collective-permute-start | bytes 3145736 | tf_op jit(solution)/shard_map/ppermute | solution.py:38
  51.6 8.3 %collective-permute-done.26.c2 = bf16[128,1024]{1,0:T(8,128)(2,1)S(1)} collective-permute-done((bf16[128,1024]{1,0:T(8,128)(2,1)S(1)}, bf16[128,1024]{1,0:T(8,128)(2,1)S(1)}, u32[]{:S(2)}, u32[]{:S(2)}) %collective-permute-start.26) | collective-permute-done | bytes 262176 | tf_op jit(solution)/shard_map/ppermute | solution.py:42
  60.0 2.3 %collective-permute-start.15 = (bf16[1,3,128,256]{3,2,1,0:T(8,128)(2,1)S(1)}, bf16[1,3,128,256]{3,2,1,0:T(8,128)(2,1)S(1)}, u32[]{:S(2)}, u32[]{:S(2)}) collective-permute-start(bf16[1,3,128,256]{3,2,1,0:T(8,128)(2,1)S(1)} %slice.38), channel_id=1, source_target_pairs={{0,64},{8,24},{16,80},{24,40},{32,96},{40,56},{48,112},{56,8},{64,... | collective-permute-start | bytes 589832 | tf_op jit(solution)/shard_map/ppermute | solution.py:542
  62.3 3.3 %collective-permute-done.27.c3 = bf16[128,1024]{1,0:T(8,128)(2,1)S(1)} collective-permute-done((bf16[128,1024]{1,0:T(8,128)(2,1)S(1)}, bf16[128,1024]{1,0:T(8,128)(2,1)S(1)}, u32[]{:S(2)}, u32[]{:S(2)}) %collective-permute-start.27) | collective-permute-done | bytes 262176 | tf_op jit(solution)/shard_map/ppermute | solution.py:42
  65.6 3.4 %collective-permute-start.16 = (bf16[1,3,128,256]{3,2,1,0:T(8,128)(2,1)S(1)}, bf16[1,3,128,256]{3,2,1,0:T(8,128)(2,1)S(1)}, u32[]{:S(2)}, u32[]{:S(2)}) collective-permute-start(bf16[1,3,128,256]{3,2,1,0:T(8,128)(2,1)S(1)} %slice.39), channel_id=1, source_target_pairs={{0,192},{8,56},{16,208},{24,8},{32,224},{40,24},{48,240},{56,40},{... | collective-permute-start | bytes 589832 | tf_op jit(solution)/shard_map/ppermute | solution.py:542
  69.0 2.7 %collective-permute-start.18 = (bf16[2,3,128,256]{3,2,1,0:T(8,128)(2,1)S(1)}, bf16[2,3,128,256]{3,2,1,0:T(8,128)(2,1)S(1)}, u32[]{:S(2)}, u32[]{:S(2)}) collective-permute-start(bf16[2,3,128,256]{3,2,1,0:T(8,128)(2,1)S(1)} %slice_bitcast_fusion), channel_id=1, source_target_pairs={{0,192},{8,56},{16,208},{24,8},{32,224},{40,24},{48,240},{56,40},{... | collective-permute-start | bytes 1179656 | tf_op jit(solution)/shard_map/ppermute | solution.py:542
  71.8 2.9 %collective-permute-start.20 = (bf16[1,3,128,256]{3,2,1,0:T(8,128)(2,1)S(1)}, bf16[1,3,128,256]{3,2,1,0:T(8,128)(2,1)S(1)}, u32[]{:S(2)}, u32[]{:S(2)}) collective-permute-start(bf16[1,3,128,256]{3,2,1,0:T(8,128)(2,1)S(1)} %slice.43), channel_id=1, source_target_pairs={{0,192},{8,56},{16,208},{24,8},{32,224},{40,24},{48,240},{56,40},{... | collective-permute-start | bytes 589832 | tf_op jit(solution)/shard_map/ppermute | solution.py:542
  77.3 3.3 %shard_map.79 = (f32[256,768]{1,0:T(8,128)S(1)}, bf16[16,2,3,128,256]{4,3,2,1,0:T(8,128)(2,1)}) custom-call(bf16[16,128,256]{2,1,0:T(8,128)(2,1)S(1)} %get-tuple-element.38.own, bf16[16,128,256]{2,1,0:T(8,128)(2,1)S(1)} %collective-permute-done.8.oth, bf16[1,2,3,128,256]{4,3,2,1,0:T(8,128)(2,1)S(1)} %get-tuple-element.68.refs_0_, ...), custom_call_target="tpu_custom_call" | custom-call | tf_op jit(solution)/shard_map/pallas_call | solution.py:427
  82.7 13.6 %all_to_all.10.agg = bf16[16,2,16,128]{3,2,1,0:T(8,128)(2,1)S(1)} all-to-all(bf16[16,2,16,128]{3,2,1,0:T(8,128)(2,1)S(1)} %get-tuple-element.42), channel_id=1, replica_groups={{0,16,32,48,64,80,96,112,128,144,160,176,192,208,224,240},{8,24,40,56,7..., dimensions={0} | all-to-all | bytes 262144 | tf_op jit(solution)/shard_map/all_to_all | solution.py:591
  98.4 9.9 %all_to_all.11.ragg = bf16[16,2,16,128]{3,2,1,0:T(8,128)(2,1)S(1)} all-to-all(bf16[16,2,16,128]{3,2,1,0:T(8,128)(2,1)S(1)} %get-tuple-element.52), channel_id=1, replica_groups={{0,16,32,48,64,80,96,112,128,144,160,176,192,208,224,240},{8,24,40,56,7..., dimensions={0} | all-to-all | bytes 262144 | tf_op jit(solution)/shard_map/all_to_all | solution.py:601
  108.3 3.6 %shard_map.85 = (bf16[128,1024]{1,0:T(8,128)(2,1)S(1)}, bf16[128,1024]{1,0:T(8,128)(2,1)S(1)}, bf16[256,768]{1,0:T(8,128)(2,1)S(1)}, f32[128,128]{1,0:T(8,128)S(1)}, f32[128,128]{1,0:T(8,128)S(1)}) custom-call(bf16[256,768]{1,0:T(8,128)(2,1)S(1)} %get-tuple-element.41.proj, f32[256,512]{1,0:T(8,128)S(1)} %get-tuple-element.51.gg, ...), custom_call_target="tpu_custom_call" | custom-call | tf_op jit(solution)/shard_map/pallas_call | solution.py:427
  112.0 3.9 %shard_map.87 = (bf16[2,128,1024]{2,1,0:T(8,128)(2,1)S(1)}, bf16[2,128,1024]{2,1,0:T(8,128)(2,1)S(1)}) custom-call(bf16[256,768]{1,0:T(8,128)(2,1)S(1)} %get-tuple-element.54.stk, bf16[16,2,3,128,256]{4,3,2,1,0:T(8,128)(2,1)} %get-tuple-element.53.wall), custom_call_target="tpu_custom_call" | custom-call | tf_op jit(solution)/shard_map/pallas_call | solution.py:427
  115.9 4.6 %collective-permute-start.31 = (bf16[2,128,1024]{2,1,0:T(8,128)(2,1)S(1)}, bf16[2,128,1024]{2,1,0:T(8,128)(2,1)S(1)}, u32[]{:S(2)}, u32[]{:S(2)}) collective-permute-start(bf16[2,128,1024]{2,1,0:T(8,128)(2,1)S(1)} %get-tuple-element.61), channel_id=1, source_target_pairs={{0,8},{8,0},{16,24},{24,16},{32,40},{40,32},{48,56},{56,48},{64,72... | collective-permute-start | bytes 1572872 | tf_op jit(solution)/shard_map/ppermute | solution.py:38
  125.6 2.6 %shard_map.86 = (bf16[128,1024]{1,0:T(8,128)(2,1)S(1)}, bf16[128,1024]{1,0:T(8,128)(2,1)S(1)}) custom-call(bf16[256,768]{1,0:T(8,128)(2,1)S(1)} %get-tuple-element.54.stk, bf16[16,2,3,128,256]{4,3,2,1,0:T(8,128)(2,1)} %get-tuple-element.53.wall), custom_call_target="tpu_custom_call" | custom-call | tf_op jit(solution)/shard_map/pallas_call | solution.py:427
  129.5 3.5 %collective-permute-start.34 = (bf16[128,1024]{1,0:T(8,128)(2,1)S(1)}, bf16[128,1024]{1,0:T(8,128)(2,1)S(1)}, u32[]{:S(2)}, u32[]{:S(2)}) collective-permute-start(bf16[128,1024]{1,0:T(8,128)(2,1)S(1)} %shard_map.89), channel_id=1, source_target_pairs={{0,4},{2,6},{4,0},{6,2},{1,5},{3,7},{5,1},{7,3},{8,12},{10,14},{12... | collective-permute-start | bytes 786440 | tf_op jit(solution)/shard_map/ppermute | solution.py:42
  133.3 6.0 %collective-permute-done.23 = bf16[128,1024]{1,0:T(8,128)(2,1)S(1)} collective-permute-done((bf16[128,1024]{1,0:T(8,128)(2,1)S(1)}, bf16[128,1024]{1,0:T(8,128)(2,1)S(1)}, u32[]{:S(2)}, u32[]{:S(2)}) %collective-permute-start.23) | collective-permute-done | bytes 262176 | tf_op jit(solution)/shard_map/ppermute | solution.py:42
  139.3 15.4 %collective-permute-done.22 = bf16[128,1024]{1,0:T(8,128)(2,1)S(1)} collective-permute-done((bf16[128,1024]{1,0:T(8,128)(2,1)S(1)}, bf16[128,1024]{1,0:T(8,128)(2,1)S(1)}, u32[]{:S(2)}, u32[]{:S(2)}) %collective-permute-start.22) | collective-permute-done | bytes 262176 | tf_op jit(solution)/shard_map/ppermute | solution.py:42
  157.1 4.8 %collective-permute-done.34.r2 = bf16[128,1024]{1,0:T(8,128)(2,1)S(1)} collective-permute-done((bf16[128,1024]{1,0:T(8,128)(2,1)S(1)}, bf16[128,1024]{1,0:T(8,128)(2,1)S(1)}, u32[]{:S(2)}, u32[]{:S(2)}) %collective-permute-start.34) | collective-permute-done | bytes 262176 | tf_op jit(solution)/shard_map/ppermute | solution.py:42
  161.8 9.1 %collective-permute-done.32.r1 = bf16[128,1024]{1,0:T(8,128)(2,1)S(1)} collective-permute-done((bf16[128,1024]{1,0:T(8,128)(2,1)S(1)}, bf16[128,1024]{1,0:T(8,128)(2,1)S(1)}, u32[]{:S(2)}, u32[]{:S(2)}) %collective-permute-start.32) | collective-permute-done | bytes 262176 | tf_op jit(solution)/shard_map/ppermute | solution.py:42
  (84 shorter events, 41.5 us)
Async XLA Ops:
  9.5 19.4 %collective-permute-start.1 = (bf16[136,1024]{1,0:T(8,128)(2,1)S(1)}, bf16[136,1024]{1,0:T(8,128)(2,1)S(1)}, u32[]{:S(2)}, u32[]{:S(2)}) collective-permute-start(bf16[136,1024]{1,0:T(8,128)(2,1)S(1)} %shard_map.77.p0.part), channel_id=1, source_target_pairs={{0,4},{2,6},{4,0},{6,2},{1,5},{3,7},{5,1},{7,3},{8,12},{10,14},{12... | collective-permute-start | bytes 835592 | tf_op jit(solution)/shard_map/ppermute | solution.py:42
  13.1 35.1 %collective-permute-start.11 = (bf16[2,2,3,128,256]{4,3,2,1,0:T(8,128)(2,1)S(1)}, bf16[2,2,3,128,256]{4,3,2,1,0:T(8,128)(2,1)S(1)}, u32[]{:S(2)}, u32[]{:S(2)}) collective-permute-start(bf16[2,2,3,128,256]{4,3,2,1,0:T(8,128)(2,1)S(1)} %pad_maximum_fusion.refs_1_), channel_id=1, source_target_pairs={{0,64},{8,24},{16,80},{24,40},{32,96},{40,56},{48,112},{56,8},{64,... | collective-permute-start | bytes 2359304 | tf_op jit(solution)/shard_map/ppermute | solution.py:542
  14.4 35.7 %collective-permute-start.12 = (bf16[2,2,3,128,256]{4,3,2,1,0:T(8,128)(2,1)S(1)}, bf16[2,2,3,128,256]{4,3,2,1,0:T(8,128)(2,1)S(1)}, u32[]{:S(2)}, u32[]{:S(2)}) collective-permute-start(bf16[2,2,3,128,256]{4,3,2,1,0:T(8,128)(2,1)S(1)} %pad_maximum_fusion.refs_1_), channel_id=1, source_target_pairs={{0,192},{8,56},{16,208},{24,8},{32,224},{40,24},{48,240},{56,40},{... | collective-permute-start | bytes 2359304 | tf_op jit(solution)/shard_map/ppermute | solution.py:542
  15.9 19.0 %collective-permute-start.2 = (bf16[136,1024]{1,0:T(8,128)(2,1)S(1)}, bf16[136,1024]{1,0:T(8,128)(2,1)S(1)}, u32[]{:S(2)}, u32[]{:S(2)}) collective-permute-start(bf16[136,1024]{1,0:T(8,128)(2,1)S(1)} %shard_map.77.p0.part), channel_id=1, source_target_pairs={{0,6},{2,0},{4,2},{6,4},{1,7},{3,1},{5,3},{7,5},{8,14},{10,8},{12,... | collective-permute-start | bytes 835592 | tf_op jit(solution)/shard_map/ppermute | solution.py:42
  16.6 19.6 %collective-permute-start.5 = (bf16[1,3,128,256]{3,2,1,0:T(8,128)(2,1)S(1)}, bf16[1,3,128,256]{3,2,1,0:T(8,128)(2,1)S(1)}, u32[]{:S(2)}, u32[]{:S(2)}) collective-permute-start(bf16[1,3,128,256]{3,2,1,0:T(8,128)(2,1)S(1)} %slice.36), channel_id=1, source_target_pairs={{0,16},{8,72},{16,32},{24,88},{32,48},{40,104},{48,0},{56,120},{64... | collective-permute-start | bytes 589832 | tf_op jit(solution)/shard_map/ppermute | solution.py:539
  28.9 14.0 %collective-permute-start.9 = (bf16[2,3,128,256]{3,2,1,0:T(8,128)(2,1)S(1)}, bf16[2,3,128,256]{3,2,1,0:T(8,128)(2,1)S(1)}, u32[]{:S(2)}, u32[]{:S(2)}) collective-permute-start(bf16[2,3,128,256]{3,2,1,0:T(8,128)(2,1)S(1)} %get-tuple-element.69), channel_id=1, source_target_pairs={{0,64},{8,24},{16,80},{24,40},{32,96},{40,56},{48,112},{56,8},{64,... | collective-permute-start | bytes 1179656 | tf_op jit(solution)/shard_map/ppermute | solution.py:542
  36.2 10.0 %collective-permute-start.10 = (bf16[2,3,128,256]{3,2,1,0:T(8,128)(2,1)S(1)}, bf16[2,3,128,256]{3,2,1,0:T(8,128)(2,1)S(1)}, u32[]{:S(2)}, u32[]{:S(2)}) collective-permute-start(bf16[2,3,128,256]{3,2,1,0:T(8,128)(2,1)S(1)} %get-tuple-element.69), channel_id=1, source_target_pairs={{0,192},{8,56},{16,208},{24,8},{32,224},{40,24},{48,240},{56,40},{... | collective-permute-start | bytes 1179656 | tf_op jit(solution)/shard_map/ppermute | solution.py:542
  42.9 33.4 %collective-permute-start.8 = (bf16[16,128,256]{2,1,0:T(8,128)(2,1)S(1)}, bf16[16,128,256]{2,1,0:T(8,128)(2,1)S(1)}, u32[]{:S(2)}, u32[]{:S(2)}) collective-permute-start(bf16[16,128,256]{2,1,0:T(8,128)(2,1)S(1)} %get-tuple-element.38.own), channel_id=1, source_target_pairs={{0,8},{8,0},{16,24},{24,16},{32,40},{40,32},{48,56},{56,48},{64,72... | collective-permute-start | bytes 3145736 | tf_op jit(solution)/shard_map/ppermute | solution.py:38
  46.3 13.7 %collective-permute-start.26 = (bf16[128,1024]{1,0:T(8,128)(2,1)S(1)}, bf16[128,1024]{1,0:T(8,128)(2,1)S(1)}, u32[]{:S(2)}, u32[]{:S(2)}) collective-permute-start(bf16[128,1024]{1,0:T(8,128)(2,1)S(1)} %bitcast.24), channel_id=1, source_target_pairs={{0,4},{2,6},{4,0},{6,2},{1,5},{3,7},{5,1},{7,3},{8,12},{10,14},{12... | collective-permute-start | bytes 786440 | tf_op jit(solution)/shard_map/ppermute | solution.py:42
  47.7 17.9 %collective-permute-start.27 = (bf16[128,1024]{1,0:T(8,128)(2,1)S(1)}, bf16[128,1024]{1,0:T(8,128)(2,1)S(1)}, u32[]{:S(2)}, u32[]{:S(2)}) collective-permute-start(bf16[128,1024]{1,0:T(8,128)(2,1)S(1)} %bitcast.25), channel_id=1, source_target_pairs={{0,6},{2,0},{4,2},{6,4},{1,7},{3,1},{5,3},{7,5},{8,14},{10,8},{12,... | collective-permute-start | bytes 786440 | tf_op jit(solution)/shard_map/ppermute | solution.py:42
  48.2 20.8 %collective-permute-start.13 = (bf16[2,3,128,256]{3,2,1,0:T(8,128)(2,1)S(1)}, bf16[2,3,128,256]{3,2,1,0:T(8,128)(2,1)S(1)}, u32[]{:S(2)}, u32[]{:S(2)}) collective-permute-start(bf16[2,3,128,256]{3,2,1,0:T(8,128)(2,1)S(1)} %constant_dynamic-update-slice_fusion), channel_id=1, source_target_pairs={{0,64},{8,24},{16,80},{24,40},{32,96},{40,56},{48,112},{56,8},{64,... | collective-permute-start | bytes 1179656 | tf_op jit(solution)/shard_map/ppermute | solution.py:542
  50.0 19.0 %collective-permute-start.14 = (bf16[2,3,128,256]{3,2,1,0:T(8,128)(2,1)S(1)}, bf16[2,3,128,256]{3,2,1,0:T(8,128)(2,1)S(1)}, u32[]{:S(2)}, u32[]{:S(2)}) collective-permute-start(bf16[2,3,128,256]{3,2,1,0:T(8,128)(2,1)S(1)} %constant_dynamic-update-slice_fusion), channel_id=1, source_target_pairs={{0,192},{8,56},{16,208},{24,8},{32,224},{40,24},{48,240},{56,40},{... | collective-permute-start | bytes 1179656 | tf_op jit(solution)/shard_map/ppermute | solution.py:542
  60.0 11.8 %collective-permute-start.15 = (bf16[1,3,128,256]{3,2,1,0:T(8,128)(2,1)S(1)}, bf16[1,3,128,256]{3,2,1,0:T(8,128)(2,1)S(1)}, u32[]{:S(2)}, u32[]{:S(2)}) collective-permute-start(bf16[1,3,128,256]{3,2,1,0:T(8,128)(2,1)S(1)} %slice.38), channel_id=1, source_target_pairs={{0,64},{8,24},{16,80},{24,40},{32,96},{40,56},{48,112},{56,8},{64,... | collective-permute-start | bytes 589832 | tf_op jit(solution)/shard_map/ppermute | solution.py:542
  69.0 11.6 %collective-permute-start.17 = (bf16[2,3,128,256]{3,2,1,0:T(8,128)(2,1)S(1)}, bf16[2,3,128,256]{3,2,1,0:T(8,128)(2,1)S(1)}, u32[]{:S(2)}, u32[]{:S(2)}) collective-permute-start(bf16[2,3,128,256]{3,2,1,0:T(8,128)(2,1)S(1)} %slice_bitcast_fusion.1), channel_id=1, source_target_pairs={{0,64},{8,24},{16,80},{24,40},{32,96},{40,56},{48,112},{56,8},{64,... | collective-permute-start | bytes 1179656 | tf_op jit(solution)/shard_map/ppermute | solution.py:542
  69.0 11.6 %collective-permute-start.18 = (bf16[2,3,128,256]{3,2,1,0:T(8,128)(2,1)S(1)}, bf16[2,3,128,256]{3,2,1,0:T(8,128)(2,1)S(1)}, u32[]{:S(2)}, u32[]{:S(2)}) collective-permute-start(bf16[2,3,128,256]{3,2,1,0:T(8,128)(2,1)S(1)} %slice_bitcast_fusion), channel_id=1, source_target_pairs={{0,192},{8,56},{16,208},{24,8},{32,224},{40,24},{48,240},{56,40},{... | collective-permute-start | bytes 1179656 | tf_op jit(solution)/shard_map/ppermute | solution.py:542
  76.3 21.1 %collective-permute-start.28 = (f32[128,256]{1,0:T(8,128)S(1)}, f32[128,256]{1,0:T(8,128)S(1)}, u32[]{:S(2)}, u32[]{:S(2)}) collective-permute-start(f32[128,256]{1,0:T(8,128)S(1)} %get-tuple-element.49), channel_id=1, source_target_pairs={{0,8},{8,0},{16,24},{24,16},{32,40},{40,32},{48,56},{56,48},{64,72... | collective-permute-start | bytes 393224 | tf_op jit(solution)/shard_map/ppermute | solution.py:38
  115.9 13.6 %collective-permute-start.31 = (bf16[2,128,1024]{2,1,0:T(8,128)(2,1)S(1)}, bf16[2,128,1024]{2,1,0:T(8,128)(2,1)S(1)}, u32[]{:S(2)}, u32[]{:S(2)}) collective-permute-start(bf16[2,128,1024]{2,1,0:T(8,128)(2,1)S(1)} %get-tuple-element.61), channel_id=1, source_target_pairs={{0,8},{8,0},{16,24},{24,16},{32,40},{40,32},{48,56},{56,48},{64,72... | collective-permute-start | bytes 1572872 | tf_op jit(solution)/shard_map/ppermute | solution.py:38
  122.4 16.9 %collective-permute-start.23 = (bf16[128,1024]{1,0:T(8,128)(2,1)S(1)}, bf16[128,1024]{1,0:T(8,128)(2,1)S(1)}, u32[]{:S(2)}, u32[]{:S(2)}) collective-permute-start(bf16[128,1024]{1,0:T(8,128)(2,1)S(1)} %shard_map.82), channel_id=1, source_target_pairs={{0,4},{2,6},{4,0},{6,2},{1,5},{3,7},{5,1},{7,3},{8,12},{10,14},{12... | collective-permute-start | bytes 786440 | tf_op jit(solution)/shard_map/ppermute | solution.py:42
  123.1 31.7 %collective-permute-start.22 = (bf16[128,1024]{1,0:T(8,128)(2,1)S(1)}, bf16[128,1024]{1,0:T(8,128)(2,1)S(1)}, u32[]{:S(2)}, u32[]{:S(2)}) collective-permute-start(bf16[128,1024]{1,0:T(8,128)(2,1)S(1)} %get-tuple-element.46), channel_id=1, source_target_pairs={{0,2},{2,4},{4,6},{6,0},{1,3},{3,5},{5,7},{7,1},{8,10},{10,12},{12... | collective-permute-start | bytes 786440 | tf_op jit(solution)/shard_map/ppermute | solution.py:42
  124.4 31.8 %collective-permute-start.24 = (bf16[128,1024]{1,0:T(8,128)(2,1)S(1)}, bf16[128,1024]{1,0:T(8,128)(2,1)S(1)}, u32[]{:S(2)}, u32[]{:S(2)}) collective-permute-start(bf16[128,1024]{1,0:T(8,128)(2,1)S(1)} %get-tuple-element.47), channel_id=1, source_target_pairs={{0,6},{2,0},{4,2},{6,4},{1,7},{3,1},{5,3},{7,5},{8,14},{10,8},{12,... | collective-permute-start | bytes 786440 | tf_op jit(solution)/shard_map/ppermute | solution.py:42
  128.2 28.8 %collective-permute-start.29 = (bf16[128,1024]{1,0:T(8,128)(2,1)S(1)}, bf16[128,1024]{1,0:T(8,128)(2,1)S(1)}, u32[]{:S(2)}, u32[]{:S(2)}) collective-permute-start(bf16[128,1024]{1,0:T(8,128)(2,1)S(1)} %get-tuple-element.56), channel_id=1, source_target_pairs={{0,8},{8,0},{16,24},{24,16},{32,40},{40,32},{48,56},{56,48},{64,72... | collective-permute-start | bytes 786440 | tf_op jit(solution)/shard_map/ppermute | solution.py:38
  129.5 32.4 %collective-permute-start.34 = (bf16[128,1024]{1,0:T(8,128)(2,1)S(1)}, bf16[128,1024]{1,0:T(8,128)(2,1)S(1)}, u32[]{:S(2)}, u32[]{:S(2)}) collective-permute-start(bf16[128,1024]{1,0:T(8,128)(2,1)S(1)} %shard_map.89), channel_id=1, source_target_pairs={{0,4},{2,6},{4,0},{6,2},{1,5},{3,7},{5,1},{7,3},{8,12},{10,14},{12... | collective-permute-start | bytes 786440 | tf_op jit(solution)/shard_map/ppermute | solution.py:42
  139.3 31.6 %collective-permute-start.32 = (bf16[128,1024]{1,0:T(8,128)(2,1)S(1)}, bf16[128,1024]{1,0:T(8,128)(2,1)S(1)}, u32[]{:S(2)}, u32[]{:S(2)}) collective-permute-start(bf16[128,1024]{1,0:T(8,128)(2,1)S(1)} %get-tuple-element.62), channel_id=1, source_target_pairs={{0,2},{2,4},{4,6},{6,0},{1,3},{3,5},{5,7},{7,1},{8,10},{10,12},{12... | collective-permute-start | bytes 786440 | tf_op jit(solution)/shard_map/ppermute | solution.py:42
  154.8 16.2 %collective-permute-start.35 = (bf16[128,1024]{1,0:T(8,128)(2,1)S(1)}, bf16[128,1024]{1,0:T(8,128)(2,1)S(1)}, u32[]{:S(2)}, u32[]{:S(2)}) collective-permute-start(bf16[128,1024]{1,0:T(8,128)(2,1)S(1)} %get-tuple-element.65), channel_id=1, source_target_pairs={{0,6},{2,0},{4,2},{6,4},{1,7},{3,1},{5,3},{7,5},{8,14},{10,8},{12,... | collective-permute-start | bytes 786440 | tf_op jit(solution)/shard_map/ppermute | solution.py:42
  (14 other events, 192.4 us)
